TPU v7x, 32 devices: a whole 2x2x4 slice. The times are simulated.
32 devices in a mesh: groups: 2 (over y), sub: 16 (over z, x, core).
Axes of the slice: x: 2, y: 2, z: 4, core: 2. Of those that a mesh axis runs over, the one named last changes fastest.
Arguments:
- samples: bfloat16 [16896, 512], P(('groups', 'sub')), parts along dimension 0, may hold values from -6 to 6
- channel_order: int32 [512], replicated, may hold values from 0 to 511, each once
- merge_table: int32 [9, 3, 256], replicated, may hold values from 0 to 128, as said below
Outputs:
- spectra: float32 [512, 4096], P(('groups', 'sub')), parts along dimension 0
There are 2 independent parts, one for each index of `groups`. A program takes and returns all parts, laid end to end along the dimension named above; an argument that names none is the same for every part. Nothing has to cross between parts.
Inputs may be any that keep to these rules, and one draw needn't show every extreme that they name: `channel_order`: a permutation of the 512 channels. `merge_table`: for level l, entry j is row d = j % 2**(l-1) of merged subband j // 2**(l-1); with C = max(1, 2**(l-2)) and e = 8, entries 0 and 1 lie in [e * (d // (2 e)), e * (d // (2 e)) + min(C, e)), and entry 2 equals entry 0 or entry 0 plus 1.
All inputs are finite; a program needn't handle non-finite values.
Results may differ from a plain program's by a relative error of at most 0.012.
Values may be sent and summed in bfloat16 or wider, within the bound.
No kernel may reach another device: no remote copies, remote signals or barrier semaphores. Data moves between devices by JAX's collectives and lax.ppermute only.
A program may use at most 64 MiB of HBM per device.

v0:
```python
import math

import jax
import jax.numpy as jnp
from jax import lax
from jax.sharding import PartitionSpec as P

LOCAL = 5
CH_DEV = 32
SAMPLES = 8192


def from_partner(block, axis, apart):
    count = lax.axis_size(axis)
    route = []
    for low in range(count):
        high = low | 1 << apart
        if high != low and high < count:
            route += [(low, high), (high, low)]
    return lax.ppermute(block, axis, route)


def delay_rows(values, shifts, margin, time_axis):
    length = values.shape[time_axis]
    moved = values
    for bit_num in range(max(1, margin.bit_length())):
        offset = 2**bit_num
        rolled = jnp.pad(moved[:, offset:], ((0, 0), (0, offset)))
        flagged = shifts >> bit_num & 1 == 1
        flagged = flagged[:, None]
        moved = jnp.where(flagged, rolled, moved)
    return moved


def merge_level(current, entries, child_rows, span_rows, time_axis):
    outputs = jnp.arange(entries.shape[1], dtype=jnp.int32)
    starts = 2 * child_rows * (outputs // span_rows)
    lower_rows = jnp.take(current, starts + entries[0], axis=1 - time_axis)
    upper_rows = jnp.take(current, starts + child_rows + entries[1], axis=1 - time_axis)
    moved_rows = delay_rows(upper_rows, entries[2], child_rows, time_axis)
    return (lower_rows.astype(jnp.float32) + moved_rows.astype(jnp.float32)).astype(jnp.bfloat16)


def spectrum(delays, channels):
    row_count = delays.shape[0]
    length = delays.shape[1]
    fold_size = length // 128
    first_index = jnp.arange(fold_size, dtype=jnp.int32)
    lane_index = jnp.arange(128, dtype=jnp.int32)
    half_index = jnp.arange(64, dtype=jnp.int32)
    angle_one = (
        2.0
        * math.pi
        / fold_size
        * (first_index[:, None] * first_index[None, :] % fold_size).astype(jnp.float32)
    )
    cos_one = jnp.cos(angle_one).astype(jnp.bfloat16)
    sin_one = jnp.sin(angle_one).astype(jnp.bfloat16)
    angle_two = (
        2.0
        * math.pi
        / length
        * (first_index[:, None] * lane_index[None, :] % length).astype(jnp.float32)
    )
    twist_cos = jnp.cos(angle_two)
    twist_sin = jnp.sin(angle_two)
    angle_three = (
        2.0 * math.pi / 128 * (lane_index[:, None] * half_index[None, :] % 128).astype(jnp.float32)
    )
    cos_three = jnp.cos(angle_three).astype(jnp.bfloat16)
    sin_three = jnp.sin(angle_three).astype(jnp.bfloat16)
    series = delays.reshape(row_count, fold_size, 128)
    first_re = jnp.einsum("kn,rnm->rkm", cos_one, series, preferred_element_type=jnp.float32)
    first_im = -jnp.einsum("kn,rnm->rkm", sin_one, series, preferred_element_type=jnp.float32)
    twisted_re = (first_re * twist_cos + first_im * twist_sin).astype(jnp.bfloat16)
    twisted_im = (first_im * twist_cos - first_re * twist_sin).astype(jnp.bfloat16)
    out_re = jnp.einsum(
        "rkn,nj->rjk", twisted_re, cos_three, preferred_element_type=jnp.float32
    ) + jnp.einsum("rkn,nj->rjk", twisted_im, sin_three, preferred_element_type=jnp.float32)
    out_im = jnp.einsum(
        "rkn,nj->rjk", twisted_im, cos_three, preferred_element_type=jnp.float32
    ) - jnp.einsum("rkn,nj->rjk", twisted_re, sin_three, preferred_element_type=jnp.float32)
    power = (out_re * out_re + out_im * out_im) / (length * channels)
    return power.reshape(row_count, 64 * fold_size)


def local(samples, channel_order, merge_table):
    owners = lax.axis_size("sub")
    owner_index = lax.axis_index("sub")
    owned_rows = CH_DEV // 2
    quarter = CH_DEV // 4
    window = samples.shape[0]
    channels = samples.shape[1]
    ordered = jnp.take(samples, channel_order, axis=1).T.reshape(owners, CH_DEV, window)
    current = lax.all_to_all(ordered, "sub", split_axis=0, concat_axis=2, tiled=True).reshape(
        CH_DEV, window * owners
    )
    for level_num in range(1, LOCAL + 1):
        entries = lax.dynamic_slice_in_dim(
            merge_table[level_num - 1], owner_index * owned_rows, owned_rows, 1
        )
        current = merge_level(
            current, entries, max(1, 2 ** (level_num - 2)), 2 ** (level_num - 1), 1
        )
    block_index = jnp.zeros((), jnp.int32)
    for bit_num in range(owners.bit_length() - 1):
        level_num = LOCAL + bit_num + 1
        half_bit = owner_index >> bit_num & 1
        block_index = block_index * 2 + half_bit
        span_rows = owned_rows * 2 ** (bit_num + 1)
        child_rows = span_rows // 2
        subband = owner_index >> bit_num + 1
        entries = lax.dynamic_slice_in_dim(
            merge_table[level_num - 1],
            subband * span_rows + owned_rows * block_index,
            owned_rows,
            1,
        )
        kept_rows = lax.dynamic_slice_in_dim(current, half_bit * quarter, quarter, 0)
        sent_rows = lax.dynamic_slice_in_dim(current, (1 - half_bit) * quarter, quarter, 0)
        partner = from_partner(sent_rows, "sub", bit_num)
        row_base = quarter * block_index
        is_low = half_bit == 0
        lower_part = jnp.where(is_low, kept_rows, partner)
        upper_part = jnp.where(is_low, partner, kept_rows)
        lower_rows = jnp.take(lower_part, entries[0] - row_base, axis=0)
        upper_rows = jnp.take(upper_part, entries[1] - row_base, axis=0)
        moved_rows = delay_rows(upper_rows, entries[2], child_rows, 1)
        current = (lower_rows.astype(jnp.float32) + moved_rows.astype(jnp.float32)).astype(
            jnp.bfloat16
        )
    return spectrum(current[:, :SAMPLES], channels)


def solution(mesh):
    in_specs = (P(("groups", "sub"), None), P(), P())
    out_specs = P(("groups", "sub"), None)
    return jax.shard_map(local, mesh=mesh, in_specs=in_specs, out_specs=out_specs, check_vma=False)
```

profile of v0, /device:TPU:0, one launch (start us, length us, event | category | flops | bytes accessed | tf_op | source)
XLA Modules:
  0.0 79.7 jit_solution(5246893528105562320)
XLA Ops:
  0.0 0.8 compare_and_fusion.18
  0.8 1.3 %copy.4 = bf16[528,512]{0,1:T(8,128)(2,1)S(1)} copy(bf16[528,512]{1,0:T(8,128)(2,1)} %param.9) | data formatting | bytes 1081344 | tf_op args[0]
  2.1 2.0 %gather_fusion = bf16[512,528]{1,0:T(8,128)(2,1)S(1)} fusion(bf16[528,512]{0,1:T(8,128)(2,1)S(1)} %copy.4, s32[1024]{0:T(1024)S(1)} %pad_clamp_fusion.18), kind=kCustom, calls=%fused_computation.18 | custom fusion | bytes 1083392 | tf_op jit(solution)/shard_map/jit(_take)/gather | solution.py:94
  4.2 1.0 %broadcast_select_fusion = bf16[512,528]{1,0:T(8,128)(2,1)} fusion(bf16[512,528]{1,0:T(8,128)(2,1)S(1)} %gather_fusion, pred[512]{0:T(512)(128)(4,1)S(1)} %compare_and_fusion.18), kind=kLoop, calls=%fused_computation.29 | loop fusion | flops 270336 | bytes 1081856 | tf_op jit(solution)/shard_map/jit(_take)/select_n | solution.py:94
  5.2 7.4 %all-to-all-start = ((bf16[16,32,528]{2,1,0:T(8,128)(2,1)}), bf16[16,32,528]{2,1,0:T(8,128)(2,1)S(1)}, u32[]{:S(2)}, u32[]{:S(2)}) async-start(bf16[16,32,528]{2,1,0:T(8,128)(2,1)} %bitcast.10), calls=%async_computation | async-start | bytes 1310720 | tf_op jit(solution)/shard_map/all_to_all | solution.py:95
  12.6 0.7 copy-done
  14.3 14.9 %all-to-all-done = bf16[16,32,528]{2,1,0:T(8,128)(2,1)S(1)} async-done(((bf16[16,32,528]{2,1,0:T(8,128)(2,1)}), bf16[16,32,528]{2,1,0:T(8,128)(2,1)S(1)}, u32[]{:S(2)}, u32[]{:S(2)}) %all-to-all-start) | async-done | bytes 540704 | tf_op jit(solution)/shard_map/all_to_all | solution.py:95
  30.0 0.7 gather_fusion.2
  30.7 0.7 gather_fusion.1
  31.9 0.7 gather_fusion.4
  32.6 0.7 gather_fusion.3
  33.8 0.7 gather_fusion.6
  34.5 0.7 gather_fusion.5
  36.0 0.7 gather_fusion.8
  36.7 0.7 gather_fusion.7
  38.5 0.7 gather_fusion.10
  39.2 0.7 gather_fusion.9
  41.5 1.2 %collective-permute-done = bf16[8,8448]{1,0:T(8,128)(2,1)S(1)} collective-permute-done((bf16[8,8448]{1,0:T(8,128)(2,1)S(1)}, bf16[8,8448]{1,0:T(8,128)(2,1)S(1)}, u32[]{:S(2)}, u32[]{:S(2)}) %collective-permute-start) | collective-permute-done | bytes 135200 | tf_op jit(solution)/shard_map/ppermute | solution.py:20
  42.7 0.7 gather_fusion.12
  44.8 0.7 gather_fusion.11
  45.8 1.3 %collective-permute-start.1 = (bf16[8,8448]{1,0:T(8,128)(2,1)S(1)}, bf16[8,8448]{1,0:T(8,128)(2,1)S(1)}, u32[]{:S(2)}, u32[]{:S(2)}) collective-permute-start(bf16[8,8448]{1,0:T(8,128)(2,1)S(1)} %constant_dynamic-slice_fusion.5), channel_id=1, source_target_pairs={{0,2},{2,0},{1,3},{3,1},{4,6},{6,4},{5,7},{7,5},{8,10},{10,8},{9,1... | collective-permute-start | bytes 405512 | tf_op jit(solution)/shard_map/ppermute | solution.py:20
  47.1 4.4 %collective-permute-done.1 = bf16[8,8448]{1,0:T(8,128)(2,1)S(1)} collective-permute-done((bf16[8,8448]{1,0:T(8,128)(2,1)S(1)}, bf16[8,8448]{1,0:T(8,128)(2,1)S(1)}, u32[]{:S(2)}, u32[]{:S(2)}) %collective-permute-start.1) | collective-permute-done | bytes 135200 | tf_op jit(solution)/shard_map/ppermute | solution.py:20
  51.6 0.7 gather_fusion.14
  54.0 0.7 gather_fusion.13
  54.9 2.3 %collective-permute-start.2 = (bf16[8,8448]{1,0:T(8,128)(2,1)S(1)}, bf16[8,8448]{1,0:T(8,128)(2,1)S(1)}, u32[]{:S(2)}, u32[]{:S(2)}) collective-permute-start(bf16[8,8448]{1,0:T(8,128)(2,1)S(1)} %constant_dynamic-slice_fusion.3), channel_id=1, source_target_pairs={{0,4},{4,0},{1,5},{5,1},{2,6},{6,2},{3,7},{7,3},{8,12},{12,8},{9,1... | collective-permute-start | bytes 405512 | tf_op jit(solution)/shard_map/ppermute | solution.py:20
  57.2 3.2 %collective-permute-done.2 = bf16[8,8448]{1,0:T(8,128)(2,1)S(1)} collective-permute-done((bf16[8,8448]{1,0:T(8,128)(2,1)S(1)}, bf16[8,8448]{1,0:T(8,128)(2,1)S(1)}, u32[]{:S(2)}, u32[]{:S(2)}) %collective-permute-start.2) | collective-permute-done | bytes 135200 | tf_op jit(solution)/shard_map/ppermute | solution.py:20
  60.5 0.7 gather_fusion.16
  63.2 0.7 gather_fusion.15
  64.3 2.5 %collective-permute-start.3 = (bf16[8,8448]{1,0:T(8,128)(2,1)S(1)}, bf16[8,8448]{1,0:T(8,128)(2,1)S(1)}, u32[]{:S(2)}, u32[]{:S(2)}) collective-permute-start(bf16[8,8448]{1,0:T(8,128)(2,1)S(1)} %constant_dynamic-slice_fusion.1), channel_id=1, source_target_pairs={{0,8},{8,0},{1,9},{9,1},{2,10},{10,2},{3,11},{11,3},{4,12},{12,4},... | collective-permute-start | bytes 405512 | tf_op jit(solution)/shard_map/ppermute | solution.py:20
  67.0 5.6 %collective-permute-done.3 = bf16[8,8448]{1,0:T(8,128)(2,1)S(1)} collective-permute-done((bf16[8,8448]{1,0:T(8,128)(2,1)S(1)}, bf16[8,8448]{1,0:T(8,128)(2,1)S(1)}, u32[]{:S(2)}, u32[]{:S(2)}) %collective-permute-start.3) | collective-permute-done | bytes 135200 | tf_op jit(solution)/shard_map/ppermute | solution.py:20
  75.5 0.7 gather_fusion.17
  78.8 0.9 %reshape.632 = f32[16,4096]{1,0:T(8,128)} reshape(f32[16,64,64]{2,1,0:T(8,128)S(1)} %fusion.5) | data formatting | bytes 524288 | tf_op jit(solution)/shard_map/reshape | solution.py:84
  (147 shorter events, 17.1 us)
Async XLA Ops:
  0.0 0.8 copy-start.1
  5.2 24.0 %all-to-all-start = ((bf16[16,32,528]{2,1,0:T(8,128)(2,1)}), bf16[16,32,528]{2,1,0:T(8,128)(2,1)S(1)}, u32[]{:S(2)}, u32[]{:S(2)}) async-start(bf16[16,32,528]{2,1,0:T(8,128)(2,1)} %bitcast.10), calls=%async_computation | async-start | bytes 1310720 | tf_op jit(solution)/shard_map/all_to_all | solution.py:95
  12.6 0.8 copy-start
  41.2 1.4 %collective-permute-start = (bf16[8,8448]{1,0:T(8,128)(2,1)S(1)}, bf16[8,8448]{1,0:T(8,128)(2,1)S(1)}, u32[]{:S(2)}, u32[]{:S(2)}) collective-permute-start(bf16[8,8448]{1,0:T(8,128)(2,1)S(1)} %constant_dynamic-slice_fusion.7), channel_id=1, source_target_pairs={{0,1},{1,0},{2,3},{3,2},{4,5},{5,4},{6,7},{7,6},{8,9},{9,8},{10,11... | collective-permute-start | bytes 405512 | tf_op jit(solution)/shard_map/ppermute | solution.py:20
  45.8 5.7 %collective-permute-start.1 = (bf16[8,8448]{1,0:T(8,128)(2,1)S(1)}, bf16[8,8448]{1,0:T(8,128)(2,1)S(1)}, u32[]{:S(2)}, u32[]{:S(2)}) collective-permute-start(bf16[8,8448]{1,0:T(8,128)(2,1)S(1)} %constant_dynamic-slice_fusion.5), channel_id=1, source_target_pairs={{0,2},{2,0},{1,3},{3,1},{4,6},{6,4},{5,7},{7,5},{8,10},{10,8},{9,1... | collective-permute-start | bytes 405512 | tf_op jit(solution)/shard_map/ppermute | solution.py:20
  54.9 5.5 %collective-permute-start.2 = (bf16[8,8448]{1,0:T(8,128)(2,1)S(1)}, bf16[8,8448]{1,0:T(8,128)(2,1)S(1)}, u32[]{:S(2)}, u32[]{:S(2)}) collective-permute-start(bf16[8,8448]{1,0:T(8,128)(2,1)S(1)} %constant_dynamic-slice_fusion.3), channel_id=1, source_target_pairs={{0,4},{4,0},{1,5},{5,1},{2,6},{6,2},{3,7},{7,3},{8,12},{12,8},{9,1... | collective-permute-start | bytes 405512 | tf_op jit(solution)/shard_map/ppermute | solution.py:20
  64.3 8.3 %collective-permute-start.3 = (bf16[8,8448]{1,0:T(8,128)(2,1)S(1)}, bf16[8,8448]{1,0:T(8,128)(2,1)S(1)}, u32[]{:S(2)}, u32[]{:S(2)}) collective-permute-start(bf16[8,8448]{1,0:T(8,128)(2,1)S(1)} %constant_dynamic-slice_fusion.1), channel_id=1, source_target_pairs={{0,8},{8,0},{1,9},{9,1},{2,10},{10,2},{3,11},{11,3},{4,12},{12,4},... | collective-permute-start | bytes 405512 | tf_op jit(solution)/shard_map/ppermute | solution.py:20
where the time goes:
time: 80.1 us; the launch traced here: 79.7 us
  waiting for transfers between devices  29.2 us (36%)
  local copies, waits for them, and re-layouts  24.4 us (30%)
  starting transfers between devices  13.7 us (17%)
  other arithmetic  9.1 us (11%)
  matrix products  2.38 us (3%)
  between operations  0.9 us (1%)
    all_to_all x1, waiting for transfers between devices, local(): lax.all_to_all(ordered, 'sub', split_axis=0, concat_axis=2, tiled=True)  14.9 us
    ppermute x4, waiting for transfers between devices, from_partner(): return lax.ppermute(block, axis, route)  14.4 us
    all_to_all x1, starting transfers between devices, local(): lax.all_to_all(ordered, 'sub', split_axis=0, concat_axis=2, tiled=True)  7.39 us
    ppermute x4, starting transfers between devices, from_partner(): return lax.ppermute(block, axis, route)  6.35 us
    slice x37, local copies, waits for them, and re-layouts, delay_rows(): rolled = jnp.pad(moved[:, offset:], ((0, 0), (0, offset)))  4.93 us
    select_n x28, other arithmetic, delay_rows(): moved = jnp.where(flagged, rolled, moved)  3.93 us
    gather x5, local copies, waits for them, and re-layouts, merge_level(): lower_rows = jnp.take(current, starts + entries[0], axis=1 - time_axis)  3.59 us
    gather x5, local copies, waits for them, and re-layouts, merge_level(): jnp.take(current, starts + child_rows + entries[1], axis=1 - time_axis)  3.59 us
  transfers between devices with their start and end apart: 5, of which 5 were waited for; matrix products, arithmetic and copies ran while one was open for 1% of the time, Pallas kernels for 0%

commit v1 on v0

--- a/solution.py
+++ b/solution.py
@@ -1,13 +1,18 @@
+import functools
 import math
 
 import jax
 import jax.numpy as jnp
+import numpy as np
 from jax import lax
+from jax.experimental import pallas as pl
+from jax.experimental.pallas import tpu as pltpu
 from jax.sharding import PartitionSpec as P
 
 LOCAL = 5
 CH_DEV = 32
 SAMPLES = 8192
+LANES = 128
 
 
 def from_partner(block, axis, apart):
@@ -21,7 +26,6 @@
 
 
 def delay_rows(values, shifts, margin, time_axis):
-    length = values.shape[time_axis]
     moved = values
     for bit_num in range(max(1, margin.bit_length())):
         offset = 2**bit_num
@@ -84,7 +88,7 @@
     return power.reshape(row_count, 64 * fold_size)
 
 
-def local(samples, channel_order, merge_table):
+def owner_plan(samples, channel_order, merge_table):
     owners = lax.axis_size("sub")
     owner_index = lax.axis_index("sub")
     owned_rows = CH_DEV // 2
@@ -132,6 +136,232 @@
     return spectrum(current[:, :SAMPLES], channels)
 
 
+def reverse_bits(value, bits):
+    flipped = 0
+    for bit_num in range(bits):
+        flipped |= (value >> bit_num & 1) << (bits - 1 - bit_num)
+    return flipped
+
+
+def tree_kernel(
+    owners, margin, samples_ref, order_ref, table_ref, out_ref, slab_ref, rows_ref, cols_ref,
+    cur_ref, pick_ref, sem,
+):
+    window, channels = samples_ref.shape
+    levels, _, dmax = table_ref.shape
+    slab = slab_ref.shape[0]
+    body = slab // LANES
+    left = margin // LANES
+    half = left // 2
+    offset = (lax.axis_index("sub") * window) % LANES
+    room = slab - window
+    zeros = jnp.zeros((room, channels), slab_ref.dtype)
+    slab_ref[:room] = zeros
+    slab_ref[window:] = zeros
+    load = pltpu.make_async_copy(
+        samples_ref, slab_ref.at[pl.ds(pl.multiple_of(offset, 16), window)], sem
+    )
+    load.start()
+
+    rows_ref[...] = jnp.zeros(rows_ref.shape, jnp.int32)
+    for level in range(levels):
+        rows_ref[3 * level : 3 * level + 3, :] = table_ref[level]
+    for part in range(channels // dmax):
+        rows_ref[3 * levels + part : 3 * levels + part + 1, :] = order_ref[
+            :, part * dmax : (part + 1) * dmax
+        ]
+    cols_ref[...] = rows_ref[...].T
+
+    raw_lane = lax.broadcasted_iota(jnp.int32, (dmax, channels), 1)
+    picks = []
+    for parity in range(2):
+        chosen = cols_ref[pl.ds(parity, dmax // 2, stride=2), :]
+        raw = jnp.concatenate(
+            [chosen[:, 3 * levels + part : 3 * levels + part + 1] for part in range(2)], axis=0
+        )
+        picks.append(jnp.where(raw == raw_lane, 1.0, 0.0).astype(jnp.bfloat16))
+    load.wait()
+    for part, pick in enumerate(picks):
+        pick_ref[part * dmax : (part + 1) * dmax, LANES * half :] = lax.dot_general(
+            pick, slab_ref[...], (((1,), (1,)), ((), ())), preferred_element_type=jnp.float32
+        )
+
+    lane = lax.broadcasted_iota(jnp.int32, (16, LANES), 1)
+    row_lane = lax.broadcasted_iota(jnp.int32, (dmax, dmax), 1)
+    row_index = lax.broadcasted_iota(jnp.int32, (dmax, 1), 0)
+    zero = jnp.zeros((16, LANES), jnp.float32)
+    for level in range(levels):
+        first, last = level == 0, level == levels - 1
+        if not first:
+            child = max(1, 2 ** (level - 1))
+            start = 2 * child * (row_index // 2**level)
+            low = start + cols_ref[:, 3 * level : 3 * level + 1]
+            high = start + child + cols_ref[:, 3 * level + 1 : 3 * level + 2]
+            current = cur_ref[...]
+            for part, index in enumerate((low, high)):
+                pick = jnp.where(index == row_lane, 1.0, 0.0).astype(jnp.bfloat16)
+                pick_ref[part * dmax : (part + 1) * dmax, :] = jnp.dot(
+                    pick, current, preferred_element_type=jnp.float32
+                )
+        for block in range(dmax // 16):
+            at = block * 16
+            reach = lane + cols_ref[at : at + 16, 3 * level + 2 : 3 * level + 3]
+            here = reach < LANES
+            source = reach & (LANES - 1)
+            low_at = pl.ds(at, 16)
+            high_at = pl.ds(dmax + at, 16)
+            after = zero
+            if last:
+                owner = reverse_bits(block, (owners - 1).bit_length())
+            for tile in reversed(range(-half if last else 0, half + body)):
+                inside = tile >= (half if first else 0)
+                at_lanes = slice(tile * LANES, (tile + 1) * LANES)
+                if inside:
+                    taken = jnp.take_along_axis(pick_ref[high_at, at_lanes], source, axis=1)
+                    total = pick_ref[low_at, at_lanes] + jnp.where(here, taken, after)
+                else:
+                    taken = zero
+                    total = jnp.where(here, taken, after)
+                after = taken
+                total = total.astype(jnp.bfloat16)
+                if last:
+                    to = tile + half
+                    out_ref[owner, :, to * LANES : (to + 1) * LANES] = total
+                else:
+                    cur_ref[at : at + 16, at_lanes] = total
+
+
+def spectrum_kernel(
+    window, margin, scale, got_ref, first_ref, cos_ref, sin_ref, third_ref, out_ref, slot_ref,
+    flat_ref,
+):
+    sources, rows, width = got_ref.shape
+    tiles = width // LANES
+    pitch = slot_ref.shape[0] // rows
+    used = sources * tiles
+    bins = first_ref.shape[0] // 2
+    halves = third_ref.shape[0] // 2
+    for source in range(sources):
+        for tile in range(tiles):
+            slot_ref[pl.ds(source * tiles + tile, rows, stride=pitch), :] = got_ref[
+                source, :, tile * LANES : (tile + 1) * LANES
+            ].astype(jnp.float32)
+    lane = lax.broadcasted_iota(jnp.int32, (halves // 2, LANES), 1)
+    sign = jnp.where(lax.broadcasted_iota(jnp.int32, (halves, LANES), 1) < bins, 1.0, -1.0)
+    for row in range(rows):
+        series = slot_ref[row * pitch : row * pitch + used, :].astype(jnp.bfloat16)
+        turned = jnp.dot(first_ref[...], series, preferred_element_type=jnp.float32)
+        real, imag = turned[:bins], turned[bins:]
+        twisted_re = (real * cos_ref[...] - imag * sin_ref[...]).astype(jnp.bfloat16)
+        twisted_im = (-imag * cos_ref[...] - real * sin_ref[...]).astype(jnp.bfloat16)
+        twisted = jnp.concatenate([twisted_re, twisted_im], axis=0)
+        mixed = lax.dot_general(
+            third_ref[...], twisted, (((1,), (1,)), ((), ())), preferred_element_type=jnp.float32
+        )
+        value = mixed[:halves] + sign * pltpu.roll(mixed[halves:], bins, axis=1)
+        square = value * value
+        power = (square + pltpu.roll(square, bins, axis=1)) * scale
+        line = jnp.where(lane < bins, power[: halves // 2], power[halves // 2 :])
+        flat_ref[
+            pl.ds(row // 8 * 8 * (halves // 2) + row % 8, halves // 2, stride=8), :
+        ] = line
+    for group in range(rows // 8):
+        for tile in range(halves // 2):
+            at = (group * (halves // 2) + tile) * 8
+            out_ref[group * 8 : group * 8 + 8, tile * LANES : (tile + 1) * LANES] = flat_ref[
+                at : at + 8, :
+            ]
+
+
+def spectrum_tables(sources, window, margin, tiles):
+    fold = SAMPLES // LANES
+    k = np.arange(fold)
+    n = np.arange(LANES)
+    m = np.arange(64)
+
+    def angle(product, period):
+        return np.float32(2.0 * math.pi / period) * (product % period).astype(np.float32)
+
+    one = angle(k[:, None] * k[None, :], fold)
+    table_one = np.concatenate([np.cos(one), np.sin(one)], axis=0)
+    first = np.zeros((2 * fold, sources * tiles), np.float32)
+    for source in range(sources):
+        start = (source * window) // LANES - margin // LANES
+        for tile in range(tiles):
+            if 0 <= start + tile < fold:
+                first[:, source * tiles + tile] = table_one[:, start + tile]
+    two = angle(k[:, None] * n[None, :], SAMPLES)
+    m = np.concatenate([m[0::2], m[1::2]])
+    three = angle(m[:, None] * n[None, :], LANES)
+    third = np.concatenate([np.cos(three), np.sin(three)], axis=0)
+    return (
+        jnp.asarray(first, jnp.bfloat16),
+        jnp.asarray(np.cos(two), jnp.float32),
+        jnp.asarray(np.sin(two), jnp.float32),
+        jnp.asarray(third, jnp.bfloat16),
+    )
+
+
+def slice_plan(samples, channel_order, merge_table):
+    owners = lax.axis_size("sub")
+    window, channels = samples.shape
+    levels, _, dmax = merge_table.shape
+    margin = window * owners - SAMPLES
+    rows = dmax // owners
+    step = math.gcd(window, LANES)
+    body = -(-(window + LANES - step) // LANES)
+    width = margin + body * LANES
+    kept = margin // 2 + body * LANES
+    vmem = pl.BlockSpec(memory_space=pltpu.VMEM)
+    partial = pl.pallas_call(
+        functools.partial(tree_kernel, owners, margin),
+        out_shape=jax.ShapeDtypeStruct((owners, rows, width), jnp.bfloat16),
+        in_specs=[pl.BlockSpec(memory_space=pl.ANY), vmem, vmem],
+        out_specs=vmem,
+        scratch_shapes=[
+            pltpu.VMEM((body * LANES, channels), jnp.bfloat16),
+            pltpu.VMEM((LANES, dmax), jnp.int32),
+            pltpu.VMEM((dmax, LANES), jnp.int32),
+            pltpu.VMEM((dmax, kept), jnp.bfloat16),
+            pltpu.VMEM((2 * dmax, kept), jnp.float32),
+            pltpu.SemaphoreType.DMA,
+        ],
+        name="tree",
+    )(samples, channel_order.reshape(1, channels), merge_table)
+    got = lax.all_to_all(partial, "sub", split_axis=0, concat_axis=0, tiled=True)
+    tables = spectrum_tables(owners, window, margin, width // LANES)
+    used = owners * width // LANES
+    pitch = used + 1
+    return pl.pallas_call(
+        functools.partial(spectrum_kernel, window, margin, 1.0 / (SAMPLES * channels)),
+        out_shape=jax.ShapeDtypeStruct((rows, SAMPLES // 2), jnp.float32),
+        in_specs=[vmem] * 5,
+        out_specs=vmem,
+        scratch_shapes=[
+            pltpu.VMEM((rows * pitch, LANES), jnp.float32),
+            pltpu.VMEM((rows * SAMPLES // 2 // LANES, LANES), jnp.float32),
+        ],
+        name="spectrum",
+    )(got, *tables)
+
+
+def local(samples, channel_order, merge_table):
+    owners = lax.axis_size("sub")
+    window, channels = samples.shape
+    dmax = merge_table.shape[2]
+    margin = window * owners - SAMPLES
+    fits = (
+        dmax == 256
+        and channels == 2 * dmax
+        and dmax == 16 * owners
+        and margin == dmax
+        and window % 16 == 0
+        and window <= 1024
+    )
+    plan = slice_plan if fits else owner_plan
+    return plan(samples, channel_order, merge_table)
+
+
 def solution(mesh):
     in_specs = (P(("groups", "sub"), None), P(), P())
     out_specs = P(("groups", "sub"), None)

time: 80.1 us -> 34.2 us (0.43)
  waiting for transfers between devices: 29.2 us -> 0 us
  local copies, waits for them, and re-layouts: 24.4 us -> 0 us
  blocking collectives: 0 us -> 20.7 us
  starting transfers between devices: 13.7 us -> 0 us
  Pallas kernels: 0 us -> 13.2 us
  other arithmetic: 9.1 us -> 0 us
  matrix products: 2.38 us -> 0 us
  between operations: 0.9 us -> 0.01 us
    all_to_all x0 -> x1, blocking collectives: none -> 20.7 us  [slice_plan(): lax.all_to_all(partial, 'sub', split_axis=0, concat_axis=0, tiled=True)]
    gather x19 -> x0, local copies, waits for them, and re-layouts: 15 us -> none  [the longest x5 3.59 us: merge_level(): lower_rows = jnp.take(current, starts + entries[0], axis=1 - time_axis)]
    all_to_all x1 -> x0, waiting for transfers between devices: 14.9 us -> none  [local(): lax.all_to_all(ordered, 'sub', split_axis=0, concat_axis=2, tiled=True)]
    ppermute x4 -> x0, waiting for transfers between devices: 14.4 us -> none  [from_partner(): return lax.ppermute(block, axis, route)]
    pallas_call x0 -> x2, Pallas kernels: none -> 13.2 us  [the longest x1 9.54 us: slice_plan(): pl.pallas_call(functools.partial(tree_kernel, owners, margin), out_shape=...]
    all_to_all x1 -> x0, starting transfers between devices: 7.39 us -> none  [local(): lax.all_to_all(ordered, 'sub', split_axis=0, concat_axis=2, tiled=True)]
    ppermute x4 -> x0, starting transfers between devices: 6.35 us -> none  [from_partner(): return lax.ppermute(block, axis, route)]
    select_n x43 -> x0, other arithmetic: 5.99 us -> none  [the longest x28 3.93 us: delay_rows(): moved = jnp.where(flagged, rolled, moved)]
  transfers between devices with their start and end apart: 5 -> 0, of which waited for: 5 -> 0; matrix products, arithmetic and copies ran while one was open for 1% -> 0% of each run, Pallas kernels for 0% -> 0%
where the time goes in v1:
time: 34.2 us; the launch traced here: 33.9 us
  blocking collectives  20.7 us (61%)
  Pallas kernels  13.2 us (39%)
    all_to_all x1, blocking collectives, slice_plan(): lax.all_to_all(partial, 'sub', split_axis=0, concat_axis=0, tiled=True)  20.7 us
    pallas_call x1, Pallas kernels, slice_plan(): pl.pallas_call(functools.partial(tree_kernel, owners, margin), out_shape=...  9.54 us
    pallas_call x1, Pallas kernels, slice_plan(): pl.pallas_call(functools.partial(spectrum_kernel, window, margin, 1.0 / (...  3.63 us

profile of v1, /device:TPU:0, one launch (start us, length us, event | category | flops | bytes accessed | tf_op | source)
XLA Modules:
  0.0 33.9 jit_solution(2815620517928291419)
XLA Ops:
  0.0 9.5 %tree.1 = bf16[16,16,896]{2,1,0:T(8,128)(2,1)} custom-call(bf16[528,512]{1,0:T(8,128)(2,1)} %samples_ref.1, s32[1,512]{1,0:T(1,128)} %bitcast.1, s32[9,3,256]{2,1,0:T(4,128)} %table_ref.1), custom_call_target="tpu_custom_call" | custom-call | tf_op jit(solution)/shard_map/tree/pallas_call | solution.py:316
  9.5 20.7 %all_to_all.5.got_ref = bf16[16,16,896]{2,1,0:T(8,128)(2,1)} all-to-all(bf16[16,16,896]{2,1,0:T(8,128)(2,1)} %tree.1), channel_id=1, replica_groups=mesh['groups'=2,'sub'=16] {'sub'}, dimensions={0} | all-to-all | bytes 917504 | tf_op jit(solution)/shard_map/all_to_all | solution.py:331
  30.3 3.6 %spectrum.1 = f32[16,4096]{1,0:T(8,128)} custom-call(bf16[16,16,896]{2,1,0:T(8,128)(2,1)} %all_to_all.5.got_ref, bf16[128,112]{1,0:T(8,128)(2,1)} %constant.8.clone.first_ref, f32[64,128]{1,0:T(8,128)} %constant.9.clone.cos_ref, f32[64,128]{1,0:T(8,128)} %constant.10.clone.sin_ref, bf16[128,128]{1,0:T(8,128)(2,1)} %constant.11.clone.third_ref), custom_call_target="tpu_custom_call" | custom-call | tf_op jit(solution)/shard_map/spectrum/pallas_call | solution.py:335

commit v2 on v1

--- a/solution.py
+++ b/solution.py
@@ -143,92 +143,154 @@
     return flipped
 
 
+def take_along(values, index, axis):
+    along = lax.GatherDimensionNumbers(
+        offset_dims=(),
+        collapsed_slice_dims=(axis,),
+        start_index_map=(axis,),
+        operand_batching_dims=(1 - axis,),
+        start_indices_batching_dims=(1 - axis,),
+    )
+    return lax.gather(
+        values, index[:, :, None], along, (1, 1), mode=lax.GatherScatterMode.PROMISE_IN_BOUNDS
+    )
+
+
 def tree_kernel(
-    owners, margin, samples_ref, order_ref, table_ref, out_ref, slab_ref, rows_ref, cols_ref,
-    cur_ref, pick_ref, sem,
+    owners, margin, samples_ref, order_ref, table_ref, out_ref, raw_ref, first_ref, pick_ref,
+    cur_ref, picked_ref, final_ref, sem,
 ):
     window, channels = samples_ref.shape
     levels, _, dmax = table_ref.shape
-    slab = slab_ref.shape[0]
-    body = slab // LANES
-    left = margin // LANES
-    half = left // 2
+    quarter = CH_DEV // 4
+    pad = margin // 2
+    length = pad + window
     offset = (lax.axis_index("sub") * window) % LANES
-    room = slab - window
-    zeros = jnp.zeros((room, channels), slab_ref.dtype)
-    slab_ref[:room] = zeros
-    slab_ref[window:] = zeros
-    load = pltpu.make_async_copy(
-        samples_ref, slab_ref.at[pl.ds(pl.multiple_of(offset, 16), window)], sem
-    )
+    load = pltpu.make_async_copy(samples_ref, raw_ref, sem)
     load.start()
 
-    rows_ref[...] = jnp.zeros(rows_ref.shape, jnp.int32)
+    final_ref[...] = jnp.zeros(final_ref.shape, final_ref.dtype)
+    lane = lax.broadcasted_iota(jnp.int32, (8, LANES), 1)
+    place = lax.broadcasted_iota(jnp.int32, (channels, LANES), 0)
+    for side in range(2):
+        for tile in range(dmax // LANES):
+            parts = [
+                take_along(
+                    jnp.broadcast_to(
+                        order_ref[:, (2 * tile + part) * LANES : (2 * tile + part + 1) * LANES],
+                        (8, LANES),
+                    ),
+                    (2 * lane + side) & (LANES - 1),
+                    1,
+                )
+                for part in range(2)
+            ]
+            chosen = jnp.where(lane < LANES // 2, parts[0], parts[1])[:1]
+            at = side * dmax + tile * LANES
+            first_ref[:, at : at + LANES] = jnp.where(place == chosen, 1.0, 0.0).astype(
+                jnp.bfloat16
+            )
+    place = lax.broadcasted_iota(jnp.int32, (dmax, dmax), 0)
+    index = lax.broadcasted_iota(jnp.int32, (1, dmax), 1)
+    for level in range(1, levels):
+        child = 2 ** (level - 1)
+        start = (index >> level) * (2 * child)
+        for side in range(2):
+            chosen = start + side * child + table_ref[level, side : side + 1, :]
+            pick_ref[level - 1, :, side * dmax : (side + 1) * dmax] = jnp.where(
+                place == chosen, 1.0, 0.0
+            ).astype(jnp.bfloat16)
+    load.wait()
+
+    row = lax.broadcasted_iota(jnp.int32, (8, LANES), 0)
+    zero = jnp.zeros((8, LANES), jnp.float32)
+    begin = pad
     for level in range(levels):
-        rows_ref[3 * level : 3 * level + 3, :] = table_ref[level]
-    for part in range(channels // dmax):
-        rows_ref[3 * levels + part : 3 * levels + part + 1, :] = order_ref[
-            :, part * dmax : (part + 1) * dmax
-        ]
-    cols_ref[...] = rows_ref[...].T
-
-    raw_lane = lax.broadcasted_iota(jnp.int32, (dmax, channels), 1)
-    picks = []
-    for parity in range(2):
-        chosen = cols_ref[pl.ds(parity, dmax // 2, stride=2), :]
-        raw = jnp.concatenate(
-            [chosen[:, 3 * levels + part : 3 * levels + part + 1] for part in range(2)], axis=0
-        )
-        picks.append(jnp.where(raw == raw_lane, 1.0, 0.0).astype(jnp.bfloat16))
-    load.wait()
-    for part, pick in enumerate(picks):
-        pick_ref[part * dmax : (part + 1) * dmax, LANES * half :] = lax.dot_general(
-            pick, slab_ref[...], (((1,), (1,)), ((), ())), preferred_element_type=jnp.float32
-        )
-
-    lane = lax.broadcasted_iota(jnp.int32, (16, LANES), 1)
-    row_lane = lax.broadcasted_iota(jnp.int32, (dmax, dmax), 1)
-    row_index = lax.broadcasted_iota(jnp.int32, (dmax, 1), 0)
-    zero = jnp.zeros((16, LANES), jnp.float32)
-    for level in range(levels):
-        first, last = level == 0, level == levels - 1
-        if not first:
-            child = max(1, 2 ** (level - 1))
-            start = 2 * child * (row_index // 2**level)
-            low = start + cols_ref[:, 3 * level : 3 * level + 1]
-            high = start + child + cols_ref[:, 3 * level + 1 : 3 * level + 2]
-            current = cur_ref[...]
-            for part, index in enumerate((low, high)):
-                pick = jnp.where(index == row_lane, 1.0, 0.0).astype(jnp.bfloat16)
-                pick_ref[part * dmax : (part + 1) * dmax, :] = jnp.dot(
-                    pick, current, preferred_element_type=jnp.float32
-                )
-        for block in range(dmax // 16):
-            at = block * 16
-            reach = lane + cols_ref[at : at + 16, 3 * level + 2 : 3 * level + 3]
-            here = reach < LANES
-            source = reach & (LANES - 1)
-            low_at = pl.ds(at, 16)
-            high_at = pl.ds(dmax + at, 16)
-            after = zero
-            if last:
-                owner = reverse_bits(block, (owners - 1).bit_length())
-            for tile in reversed(range(-half if last else 0, half + body)):
-                inside = tile >= (half if first else 0)
-                at_lanes = slice(tile * LANES, (tile + 1) * LANES)
-                if inside:
-                    taken = jnp.take_along_axis(pick_ref[high_at, at_lanes], source, axis=1)
-                    total = pick_ref[low_at, at_lanes] + jnp.where(here, taken, after)
+        last = level == levels - 1
+        if level:
+            picked_ref[begin:length, :] = jnp.dot(
+                cur_ref[begin:length, :], pick_ref[level - 1], preferred_element_type=jnp.float32
+            )
+        else:
+            picked_ref[begin:length, :] = jnp.dot(
+                raw_ref[...], first_ref[...], preferred_element_type=jnp.float32
+            )
+        reached = (pad - 2**level) // 16 * 16
+        for tile in range(dmax // LANES):
+            output = tile * LANES + lane
+            steps = (output & (2**level - 1)) // (2 * quarter)
+            least = (tile * LANES & (2**level - 1)) // (2 * quarter)
+            most = ((tile * LANES + LANES - 1) & (2**level - 1)) // (2 * quarter)
+            if 2**level <= LANES:
+                least, most = 0, (2**level - 1) // (2 * quarter)
+            bits = (most - least).bit_length()
+            shift = jnp.broadcast_to(
+                table_ref[level, 2:3, tile * LANES : (tile + 1) * LANES], (8, LANES)
+            )
+            rest = row + shift - steps * quarter
+            here = rest < 8
+            source = rest & 7
+            flags = [((steps - least) >> bit & 1) == 1 for bit in range(bits)]
+            known = {}
+
+            def coarse(bit, at):
+                if at >= length // 8:
+                    return None
+                if (bit, at) not in known:
+                    if bit == 0:
+                        known[bit, at] = (
+                            picked_ref[
+                                at * 8 : at * 8 + 8,
+                                dmax + tile * LANES : dmax + (tile + 1) * LANES,
+                            ]
+                            if at * 8 >= begin
+                            else None
+                        )
+                    else:
+                        near, far = coarse(bit - 1, at), coarse(bit - 1, at + 2 ** (bit - 1))
+                        if near is None and far is None:
+                            known[bit, at] = None
+                        else:
+                            near = zero if near is None else near
+                            far = zero if far is None else far
+                            known[bit, at] = jnp.where(flags[bit - 1], far, near)
+                return known[bit, at]
+
+            def fine(at):
+                if ("fine", at) not in known:
+                    value = coarse(bits, at + least)
+                    known["fine", at] = None if value is None else take_along(value, source, 0)
+                return known["fine", at]
+
+            def merged(at):
+                near, far = fine(at), fine(at + 1)
+                total = None
+                if near is not None or far is not None:
+                    total = jnp.where(
+                        here, zero if near is None else near, zero if far is None else far
+                    )
+                if begin <= at * 8:
+                    low = picked_ref[at * 8 : at * 8 + 8, tile * LANES : (tile + 1) * LANES]
+                    total = low if total is None else low + total
+                return zero if total is None else total
+
+            lanes = slice(tile * LANES, (tile + 1) * LANES)
+            for at in range(reached // 8, length // 8, 2):
+                both = jnp.concatenate([merged(at), merged(at + 1)], axis=0).astype(jnp.bfloat16)
+                if last:
+                    to = pl.multiple_of(offset + at * 8 + pad, 16)
+                    final_ref[pl.ds(to, 16), lanes] = both
                 else:
-                    taken = zero
-                    total = jnp.where(here, taken, after)
-                after = taken
-                total = total.astype(jnp.bfloat16)
-                if last:
-                    to = tile + half
-                    out_ref[owner, :, to * LANES : (to + 1) * LANES] = total
-                else:
-                    cur_ref[at : at + 16, at_lanes] = total
+                    cur_ref[at * 8 : at * 8 + 16, lanes] = both
+        begin = max(reached, 0)
+
+    for tile in range(dmax // LANES):
+        for time in range(final_ref.shape[0] // LANES):
+            lanes = slice(time * LANES, (time + 1) * LANES)
+            turned = final_ref[lanes, tile * LANES : (tile + 1) * LANES].T
+            for block in range(LANES // 16):
+                owner = reverse_bits(tile * (LANES // 16) + block, (owners - 1).bit_length())
+                out_ref[owner, :, lanes] = turned[block * 16 : (block + 1) * 16]
 
 
 def spectrum_kernel(
@@ -311,7 +373,7 @@
     step = math.gcd(window, LANES)
     body = -(-(window + LANES - step) // LANES)
     width = margin + body * LANES
-    kept = margin // 2 + body * LANES
+    kept = margin // 2 + window
     vmem = pl.BlockSpec(memory_space=pltpu.VMEM)
     partial = pl.pallas_call(
         functools.partial(tree_kernel, owners, margin),
@@ -319,11 +381,12 @@
         in_specs=[pl.BlockSpec(memory_space=pl.ANY), vmem, vmem],
         out_specs=vmem,
         scratch_shapes=[
-            pltpu.VMEM((body * LANES, channels), jnp.bfloat16),
-            pltpu.VMEM((LANES, dmax), jnp.int32),
-            pltpu.VMEM((dmax, LANES), jnp.int32),
-            pltpu.VMEM((dmax, kept), jnp.bfloat16),
-            pltpu.VMEM((2 * dmax, kept), jnp.float32),
+            pltpu.VMEM((window, channels), jnp.bfloat16),
+            pltpu.VMEM((channels, 2 * dmax), jnp.bfloat16),
+            pltpu.VMEM((levels - 1, dmax, 2 * dmax), jnp.bfloat16),
+            pltpu.VMEM((kept, dmax), jnp.bfloat16),
+            pltpu.VMEM((kept, 2 * dmax), jnp.float32),
+            pltpu.VMEM((width, dmax), jnp.bfloat16),
             pltpu.SemaphoreType.DMA,
         ],
         name="tree",

time: 34.2 us -> 29.2 us (0.85)
  Pallas kernels: 13.2 us -> 8.12 us
    pallas_call x1, Pallas kernels: 9.54 us -> 4.49 us  [slice_plan(): pl.pallas_call(functools.partial(tree_kernel, owners, margin), out_shape=...]
where the time goes in v2:
time: 29.2 us; the launch traced here: 28.9 us
  blocking collectives  20.7 us (71%)
  Pallas kernels  8.12 us (28%)
    all_to_all x1, blocking collectives, slice_plan(): lax.all_to_all(partial, 'sub', split_axis=0, concat_axis=0, tiled=True)  20.7 us
    pallas_call x1, Pallas kernels, slice_plan(): pl.pallas_call(functools.partial(tree_kernel, owners, margin), out_shape=...  4.49 us
    pallas_call x1, Pallas kernels, slice_plan(): pl.pallas_call(functools.partial(spectrum_kernel, window, margin, 1.0 / (...  3.63 us

profile of v2, /device:TPU:0, one launch (start us, length us, event | category | flops | bytes accessed | tf_op | source)
XLA Modules:
  0.0 28.9 jit_solution(8064084850205630465)
XLA Ops:
  0.0 4.5 %tree.1 = bf16[16,16,896]{2,1,0:T(8,128)(2,1)} custom-call(bf16[528,512]{1,0:T(8,128)(2,1)} %samples_ref.1, s32[1,512]{1,0:T(1,128)} %bitcast.1, s32[9,3,256]{2,1,0:T(4,128)} %table_ref.1), custom_call_target="tpu_custom_call" | custom-call | tf_op jit(solution)/shard_map/tree/pallas_call | solution.py:378
  4.5 20.7 %all_to_all.5.got_ref = bf16[16,16,896]{2,1,0:T(8,128)(2,1)} all-to-all(bf16[16,16,896]{2,1,0:T(8,128)(2,1)} %tree.1), channel_id=1, replica_groups=mesh['groups'=2,'sub'=16] {'sub'}, dimensions={0} | all-to-all | bytes 917504 | tf_op jit(solution)/shard_map/all_to_all | solution.py:394
  25.2 3.6 %spectrum.1 = f32[16,4096]{1,0:T(8,128)} custom-call(bf16[16,16,896]{2,1,0:T(8,128)(2,1)} %all_to_all.5.got_ref, bf16[128,112]{1,0:T(8,128)(2,1)} %constant.8.clone.first_ref, f32[64,128]{1,0:T(8,128)} %constant.9.clone.cos_ref, f32[64,128]{1,0:T(8,128)} %constant.10.clone.sin_ref, bf16[128,128]{1,0:T(8,128)(2,1)} %constant.11.clone.third_ref), custom_call_target="tpu_custom_call" | custom-call | tf_op jit(solution)/shard_map/spectrum/pallas_call | solution.py:398

commit v3 on v2

--- a/solution.py
+++ b/solution.py
@@ -295,7 +295,7 @@
 
 def spectrum_kernel(
     window, margin, scale, got_ref, first_ref, cos_ref, sin_ref, third_ref, out_ref, slot_ref,
-    flat_ref,
+    flat_ref, lines_ref, sems,
 ):
     sources, rows, width = got_ref.shape
     tiles = width // LANES
@@ -310,6 +310,7 @@
             ].astype(jnp.float32)
     lane = lax.broadcasted_iota(jnp.int32, (halves // 2, LANES), 1)
     sign = jnp.where(lax.broadcasted_iota(jnp.int32, (halves, LANES), 1) < bins, 1.0, -1.0)
+    stores = []
     for row in range(rows):
         series = slot_ref[row * pitch : row * pitch + used, :].astype(jnp.bfloat16)
         turned = jnp.dot(first_ref[...], series, preferred_element_type=jnp.float32)
@@ -327,12 +328,23 @@
         flat_ref[
             pl.ds(row // 8 * 8 * (halves // 2) + row % 8, halves // 2, stride=8), :
         ] = line
-    for group in range(rows // 8):
-        for tile in range(halves // 2):
-            at = (group * (halves // 2) + tile) * 8
-            out_ref[group * 8 : group * 8 + 8, tile * LANES : (tile + 1) * LANES] = flat_ref[
-                at : at + 8, :
-            ]
+        if row % 8 == 7:
+            group = row // 8
+            for tile in range(halves // 2):
+                at = (group * (halves // 2) + tile) * 8
+                lines_ref[group * 8 : group * 8 + 8, tile * LANES : (tile + 1) * LANES] = flat_ref[
+                    at : at + 8, :
+                ]
+            stores.append(
+                pltpu.make_async_copy(
+                    lines_ref.at[pl.ds(group * 8, 8)],
+                    out_ref.at[pl.ds(group * 8, 8)],
+                    sems.at[group],
+                )
+            )
+            stores[-1].start()
+    for store in stores:
+        store.wait()
 
 
 def spectrum_tables(sources, window, margin, tiles):
@@ -377,7 +389,7 @@
     vmem = pl.BlockSpec(memory_space=pltpu.VMEM)
     partial = pl.pallas_call(
         functools.partial(tree_kernel, owners, margin),
-        out_shape=jax.ShapeDtypeStruct((owners, rows, width), jnp.bfloat16),
+        out_shape=pltpu.VMEM((owners, rows, width), jnp.bfloat16),
         in_specs=[pl.BlockSpec(memory_space=pl.ANY), vmem, vmem],
         out_specs=vmem,
         scratch_shapes=[
@@ -392,17 +404,23 @@
         name="tree",
     )(samples, channel_order.reshape(1, channels), merge_table)
     got = lax.all_to_all(partial, "sub", split_axis=0, concat_axis=0, tiled=True)
-    tables = spectrum_tables(owners, window, margin, width // LANES)
+    got = pltpu.with_memory_space_constraint(got, pltpu.VMEM)
+    tables = [
+        pltpu.with_memory_space_constraint(table, pltpu.VMEM)
+        for table in spectrum_tables(owners, window, margin, width // LANES)
+    ]
     used = owners * width // LANES
     pitch = used + 1
     return pl.pallas_call(
         functools.partial(spectrum_kernel, window, margin, 1.0 / (SAMPLES * channels)),
         out_shape=jax.ShapeDtypeStruct((rows, SAMPLES // 2), jnp.float32),
         in_specs=[vmem] * 5,
-        out_specs=vmem,
+        out_specs=pl.BlockSpec(memory_space=pl.ANY),
         scratch_shapes=[
             pltpu.VMEM((rows * pitch, LANES), jnp.float32),
             pltpu.VMEM((rows * SAMPLES // 2 // LANES, LANES), jnp.float32),
+            pltpu.VMEM((rows, SAMPLES // 2), jnp.float32),
+            pltpu.SemaphoreType.DMA((rows // 8,)),
         ],
         name="spectrum",
     )(got, *tables)

time: 29.2 us -> 27.2 us (0.932)
  Pallas kernels: 8.12 us -> 6.26 us
    pallas_call x1, Pallas kernels: 3.63 us -> 2.55 us  [slice_plan(): pl.pallas_call(functools.partial(spectrum_kernel, window, margin, 1.0 / (...]
    pallas_call x1, Pallas kernels: 4.49 us -> 3.72 us  [slice_plan(): pl.pallas_call(functools.partial(tree_kernel, owners, margin), out_shape=...]
where the time goes in v3:
time: 27.2 us; the launch traced here: 26.9 us
  blocking collectives  20.5 us (75%)
  Pallas kernels  6.26 us (23%)
    all_to_all x1, blocking collectives, slice_plan(): lax.all_to_all(partial, 'sub', split_axis=0, concat_axis=0, tiled=True)  20.5 us
    pallas_call x1, Pallas kernels, slice_plan(): pl.pallas_call(functools.partial(tree_kernel, owners, margin), out_shape=...  3.72 us
    pallas_call x1, Pallas kernels, slice_plan(): pl.pallas_call(functools.partial(spectrum_kernel, window, margin, 1.0 / (...  2.55 us

profile of v3, /device:TPU:0, one launch (start us, length us, event | category | flops | bytes accessed | tf_op | source)
XLA Modules:
  0.0 26.9 jit_solution(10171615590688239411)
XLA Ops:
  0.0 3.7 %tree.1 = bf16[16,16,896]{2,1,0:T(8,128)(2,1)S(1)} custom-call(bf16[528,512]{1,0:T(8,128)(2,1)} %samples_ref.1, s32[1,512]{1,0:T(1,128)} %bitcast.1, s32[9,3,256]{2,1,0:T(4,128)} %table_ref.1), custom_call_target="tpu_custom_call" | custom-call | tf_op jit(solution)/shard_map/tree/pallas_call | solution.py:390
  3.7 0.0 copy-start
  3.7 0.0 copy-start.1
  3.7 0.0 copy-start.2
  3.8 0.0 copy-start.3
  3.8 20.5 %all_to_all.5.got_ref = bf16[16,16,896]{2,1,0:T(8,128)(2,1)S(1)} all-to-all(bf16[16,16,896]{2,1,0:T(8,128)(2,1)S(1)} %tree.1), channel_id=1, replica_groups=mesh['groups'=2,'sub'=16] {'sub'}, dimensions={0} | all-to-all | bytes 917504 | tf_op jit(solution)/shard_map/all_to_all | solution.py:406
  24.3 0.0 copy-done
  24.3 0.0 copy-done.1
  24.3 0.0 copy-done.2
  24.3 0.0 copy-done.3
  24.3 2.5 %spectrum.1 = f32[16,4096]{1,0:T(8,128)} custom-call(bf16[16,16,896]{2,1,0:T(8,128)(2,1)S(1)} %all_to_all.5.got_ref, bf16[128,112]{1,0:T(8,128)(2,1)S(1)} %copy-done.3, f32[64,128]{1,0:T(8,128)S(1)} %copy-done.2, f32[64,128]{1,0:T(8,128)S(1)} %copy-done.1, bf16[128,128]{1,0:T(8,128)(2,1)S(1)} %copy-done), custom_call_target="tpu_custom_call" | custom-call | tf_op jit(solution)/shard_map/spectrum/pallas_call | solution.py:414
Async XLA Ops:
  3.7 20.6 %copy-start = (bf16[128,128]{1,0:T(8,128)(2,1)S(1)}, bf16[128,128]{1,0:T(8,128)(2,1)}, u32[]{:S(2)}) copy-start(bf16[128,128]{1,0:T(8,128)(2,1)} %constant.11.clone.third_ref) | copy-start | bytes 98308
  3.7 20.6 %copy-start.1 = (f32[64,128]{1,0:T(8,128)S(1)}, f32[64,128]{1,0:T(8,128)}, u32[]{:S(2)}) copy-start(f32[64,128]{1,0:T(8,128)} %constant.10.clone.sin_ref) | copy-start | bytes 98308
  3.7 20.6 %copy-start.2 = (f32[64,128]{1,0:T(8,128)S(1)}, f32[64,128]{1,0:T(8,128)}, u32[]{:S(2)}) copy-start(f32[64,128]{1,0:T(8,128)} %constant.9.clone.cos_ref) | copy-start | bytes 98308
  3.8 20.6 %copy-start.3 = (bf16[128,112]{1,0:T(8,128)(2,1)S(1)}, bf16[128,112]{1,0:T(8,128)(2,1)}, u32[]{:S(2)}) copy-start(bf16[128,112]{1,0:T(8,128)(2,1)} %constant.8.clone.first_ref) | copy-start | bytes 86020
